TPU v7x, 32 devices: a whole 2x2x4 slice. The times are simulated.
32 devices in a mesh: dp: 4 (over y, x), ctx: 2 (over core), tp: 4 (over z).
Axes of the slice: x: 2, y: 2, z: 4, core: 2. Of those that a mesh axis runs over, the one named last changes fastest.
Arguments:
- tokens: bfloat16 [4, 1024, 4096], P('dp', ('ctx', 'tp')), may hold values from -6 to 6
- norm_gain: float32 [4096], replicated, may hold values from 0.1 to 1.9
- w_qkv: bfloat16 [4096, 3, 4096], P(None, None, 'tp'), may hold values from -8 to 8, as said below
- sub_gain: float32 [4096], P('tp'), may hold values from 0.1 to 1.9
- w_out: bfloat16 [4096, 4096], P('tp'), may hold values from -8 to 8, as said below
Outputs:
- block_out: bfloat16 [4, 1024, 4096], P('dp', ('ctx', 'tp'))
Inputs may be any that keep to these rules, and one draw needn't show every extreme that they name: For each m, no entry of w_qkv[:, m, :] has a magnitude between 0.35 and 3 times half the mean magnitude of w_qkv[:, m, :]. No entry of w_out has a magnitude between 0.35 and 3 times half the mean magnitude of w_out.
All inputs are finite; a program needn't handle non-finite values.
Results may differ from a plain program's by a relative error of at most 0.012.
Values may be sent and summed in bfloat16 or wider, within the bound.
A program may use at most 192 MiB of HBM per device.

v0:
```python
import jax
import jax.numpy as jnp
from jax import lax
from jax.sharding import PartitionSpec as P

D = 4096
H = 32
HD = 128


eps_norm = 1e-05
low_value = -1e30


def quantize(weight, scale):
    ratio = weight.astype(jnp.float32) / scale
    ternary = jnp.where(ratio > 0.5, 1.0, jnp.where(ratio < -0.5, -1.0, 0.0))
    return (scale * ternary).astype(jnp.bfloat16)


def attend_tiles(state, q_tiles, q_places, key_piece, value_piece):
    rows = key_piece.shape[0]
    heads_local = key_piece.shape[1]
    q_block = q_tiles.shape[1]
    key_count = rows // q_block
    key_tiles = key_piece.reshape(key_count, q_block, heads_local, HD)
    value_tiles = value_piece.reshape(key_count, q_block, heads_local, HD)
    inv_root = 1.0 / jnp.sqrt(jnp.float32(HD))

    def one_block(bundle):
        q_one, pos_one, top_old, total_old, acc_old = bundle
        last_place = pos_one[q_block - 1]

        def one_key(index, carried):
            key_start = index * q_block

            def compute(running):
                top_run, total_run, acc_run = running
                key_one = lax.dynamic_index_in_dim(key_tiles, index, 0, keepdims=False)
                value_one = lax.dynamic_index_in_dim(value_tiles, index, 0, keepdims=False)
                key_places = key_start + jnp.arange(q_block, dtype=jnp.int32)
                score = (
                    jnp.einsum("qhd,khd->qhk", q_one, key_one, preferred_element_type=jnp.float32)
                    * inv_root
                )
                allowed = key_places[None, None, :] <= pos_one[:, None, None]
                score = jnp.where(allowed, score, low_value)
                top_new = jnp.maximum(top_run, jnp.max(score, axis=-1))
                expo = jnp.where(allowed, jnp.exp(score - top_new[..., None]), 0.0)
                factor = jnp.exp(top_run - top_new)
                total_new = total_run * factor + jnp.sum(expo, axis=-1)
                acc_new = acc_run * factor[..., None] + jnp.einsum(
                    "qhk,khd->qhd",
                    expo.astype(jnp.bfloat16),
                    value_one,
                    preferred_element_type=jnp.float32,
                )
                return (top_new, total_new, acc_new)

            return lax.cond(key_start <= last_place, compute, lambda running: running, carried)

        return lax.fori_loop(0, key_count, one_key, (top_old, total_old, acc_old))

    return lax.map(one_block, (q_tiles, q_places, state[0], state[1], state[2]))


def body(tokens, norm_gain, w_qkv, sub_gain, w_out):
    model_width = tokens.shape[2]
    head_cols = w_qkv.shape[2]
    heads_local = head_cols // HD
    count = float(D * H * HD)
    ctx_index = lax.axis_index("ctx")
    inputs = tokens[0].astype(jnp.float32)
    normed = (
        inputs * lax.rsqrt(jnp.mean(inputs * inputs, axis=-1, keepdims=True) + eps_norm) * norm_gain
    ).astype(jnp.bfloat16)
    qkv_abs = jnp.sum(jnp.abs(w_qkv), axis=(0, 2), dtype=jnp.float32)
    out_abs = jnp.sum(jnp.abs(w_out), dtype=jnp.float32)
    qkv_total = lax.psum(qkv_abs, "tp")
    out_total = out_abs
    qkv_scale = qkv_total / count
    w_in = quantize(w_qkv, qkv_scale[None, :, None]).reshape(model_width, 3 * head_cols)
    qkv = jnp.dot(
        lax.all_gather(normed, "tp", axis=0, tiled=True), w_in, preferred_element_type=jnp.float32
    ).astype(jnp.bfloat16)
    block_rows = qkv.shape[0]
    half_rows = block_rows // 2
    q_block = min(512, half_rows)
    q_count = block_rows // q_block
    query = qkv[:, :head_cols]
    keys = qkv[:, head_cols : 2 * head_cols].reshape(block_rows, heads_local, HD)
    values = qkv[:, 2 * head_cols :].reshape(block_rows, heads_local, HD)
    local_places = jnp.arange(block_rows, dtype=jnp.int32)
    q_flat = ctx_index * block_rows + local_places
    q_tiles = query.reshape(q_count, q_block, heads_local, HD)
    q_places = q_flat.reshape(q_count, q_block)
    initial = (
        jnp.full((q_count, q_block, heads_local), low_value, jnp.float32),
        jnp.zeros((q_count, q_block, heads_local), jnp.float32),
        jnp.zeros((q_count, q_block, heads_local, HD), jnp.float32),
    )
    state = attend_tiles(
        initial,
        q_tiles,
        q_places,
        lax.all_gather(keys, "ctx", axis=0, tiled=True),
        lax.all_gather(values, "ctx", axis=0, tiled=True),
    )
    attended = (state[2] / state[1][..., None]).reshape(block_rows, head_cols)
    row_sums = jnp.sum(attended * attended, axis=-1)
    power = lax.psum(row_sums, "tp") / float(H * HD)
    out_total = lax.psum(out_total, "tp")
    w_o = quantize(w_out, out_total / count)
    sub_normed = (attended * lax.rsqrt(power + eps_norm)[:, None] * sub_gain).astype(jnp.bfloat16)
    projected = lax.psum_scatter(
        jnp.dot(sub_normed, w_o, preferred_element_type=jnp.float32).astype(jnp.bfloat16),
        "tp",
        scatter_dimension=0,
        tiled=True,
    ).astype(jnp.float32)
    return (inputs + projected).astype(jnp.bfloat16)[None]


def solution(mesh):
    return jax.shard_map(
        body,
        mesh=mesh,
        in_specs=(P("dp", ("ctx", "tp"), None), P(), P(None, None, "tp"), P("tp"), P("tp", None)),
        out_specs=P("dp", ("ctx", "tp"), None),
        check_vma=False,
    )
```

profile of v0, /device:TPU:15, one launch (start us, length us, event | category | flops | bytes accessed | tf_op | source)
XLA Modules:
  0.0 302.2 jit_solution(9778151256732178157)
XLA Ops:
  6.5 1.5 fusion.22
  8.1 2.5 fusion.24
  10.7 15.6 %convert_reduce_fusion = f32[3]{0:T(128)S(1)} fusion(bf16[4096,3,1024]{2,0,1:T(8,128)(2,1)} %param.13), kind=kLoop, calls=%fused_computation.33 | loop fusion | flops 37748732 | bytes 25165836 | tf_op jit(solution)/shard_map/reduce_sum | solution.py:77
  26.2 33.4 %copy.15 = bf16[4096,3,1024]{0,2,1:T(8,128)(2,1)} copy(bf16[4096,3,1024]{2,0,1:T(8,128)(2,1)} %param.13) | data formatting | bytes 50331648 | tf_op args[2]
  59.7 8.0 %psum.21 = f32[3]{0:T(128)S(1)} all-reduce(f32[3]{0:T(128)S(1)} %convert_reduce_fusion), channel_id=1, replica_groups=mesh['dp'=4,'ctx'=2,'tp'=4] {'tp'}, use_global_device_ids=true, to_apply=%region_2.0 | all-reduce | flops 3 | bytes 24 | tf_op jit(solution)/shard_map/psum | solution.py:79
  67.7 25.8 %multiply_convert_fusion = bf16[4096,3,1024]{0,2,1:T(8,128)(2,1)} fusion(bf16[4096,3,1024]{0,2,1:T(8,128)(2,1)} %copy.15, f32[3]{0:T(128)S(1)} %broadcast_multiply_fusion), kind=kLoop, calls=%fused_computation.31 | loop fusion | flops 100663296 | bytes 50331660 | tf_op jit(solution)/shard_map/convert_element_type | solution.py:18
  93.4 20.4 %convolution_convert_fusion = bf16[512,3072]{1,0:T(8,128)(2,1)} fusion(bf16[512,4096]{1,0:T(8,128)(2,1)} %all-gather.4.cloned.1.call-done, bf16[4096,3072]{0,1:T(8,128)(2,1)} %bitcast.77), kind=kOutput, calls=%fused_computation.39 | convolution fusion | flops 12886474752 | bytes 32505856 | tf_op jit(solution)/shard_map/dot_general | solution.py:83
  113.8 2.6 slice_bitcast_fusion
  116.4 1.2 copy.23
  117.7 1.3 copy.24
  119.2 8.3 %convert_reduce_fusion.1 = f32[]{:T(128)} fusion(bf16[1024,4096]{1,0:T(8,128)(2,1)} %param.15), kind=kLoop, calls=%fused_computation.36 | loop fusion | flops 12582911 | bytes 8388612 | tf_op jit(solution)/shard_map/reduce_sum | solution.py:78
  127.8 4.5 %all-gather.6.cloned.1.call-done = bf16[1024,8,128]{2,1,0:T(8,128)(2,1)} async-done(((bf16[512,8,128]{2,1,0:T(8,128)(2,1)}), bf16[1024,8,128]{2,1,0:T(8,128)(2,1)}) %all-gather.6.cloned.1.call-update) | async-done | bytes 2097168 | tf_op jit(solution)/shard_map/all_gather | solution.py:106
  132.3 2.1 copy.17
  134.4 11.2 %all-gather.8.cloned.1.call-done = bf16[1024,8,128]{2,1,0:T(8,128)(2,1)} async-done(((bf16[512,8,128]{2,1,0:T(8,128)(2,1)}), bf16[1024,8,128]{2,1,0:T(8,128)(2,1)}) %all-gather.8.cloned.1.call-update) | async-done | bytes 2097168 | tf_op jit(solution)/shard_map/all_gather | solution.py:107
  145.7 4.3 %copy.18 = bf16[4,256,8,128]{1,3,2,0:T(8,128)(2,1)} copy(bf16[4,256,8,128]{3,2,1,0:T(8,128)(2,1)} %bitcast.82) | data formatting | bytes 4194304 | tf_op jit(solution)/shard_map/while | solution.py:64
  149.9 44.3 %while.30 = (s32[]{:T(128)}, f32[2,256,8]{1,2,0:T(8,128)S(1)}, f32[2,256,8,128]{1,3,2,0:T(8,128)}, s32[2,256]{1,0:T(2,128)S(1)}, bf16[2,256,8,128]{3,2,1,0:T(8,1...) while((s32[]{:T(128)}, f32[2,256,8]{1,2,0:T(8,128)S(1)}, ...), condition=%wide.region_10.11_spmd, body=%wide.region_3.10_spmd.sunk | while | flops 275845376 | bytes 32413880 | solution.py:64
  149.9 0.7 dynamic-slice.2
  151.0 1.1 squeeze.35
  152.1 15.5 %while.31 = (s32[]{:T(128)}, f32[256,8]{0,1:T(8,128)S(1)}, f32[256,8]{0,1:T(8,128)S(1)}, f32[256,8,128]{0,2,1:T(8,128)}, s32[]{:T(128)}, /*index=5*/s32[256]{0:T...) while((s32[]{:T(128)}, f32[256,8]{0,1:T(8,128)S(1)}, ...), condition=%wide.region_9.9_spmd, body=%wide.region_4.8_spmd.sunk | while | flops 275845376 | bytes 18746732 | solution.py:62
  152.8 4.2 %conditional.2 = ((f32[256,8]{0,1:T(8,128)S(1)}, f32[256,8]{0,1:T(8,128)S(1)}, f32[256,8,128]{0,2,1:T(8,128)})) conditional(s32[]{:T(128)} %convert_element_type.97, (f32[256,8]{0,1:T(8,128)S(1)}, f32[256,8]{0,1:T(8,128)S(1)}, f32[256,8,128]{0,2,1:T(8,128)}) %tuple.61, (s32[]{:T(128)}, s32[256]{0:T(256)S(1)}, s32[]{:T(128)}, ...), branch_computations={%region_5.4_spmd, %region_6.7_spmd} | conditional | flops 275845376 | bytes 18746502 | solution.py:60
  152.9 0.5 fusion
  153.4 0.5 fusion.2
  154.1 1.9 fusion.3
  156.0 1.0 copy-done.1
  157.7 4.2 %conditional.2 = ((f32[256,8]{0,1:T(8,128)S(1)}, f32[256,8]{0,1:T(8,128)S(1)}, f32[256,8,128]{0,2,1:T(8,128)})) conditional(s32[]{:T(128)} %convert_element_type.97, (f32[256,8]{0,1:T(8,128)S(1)}, f32[256,8]{0,1:T(8,128)S(1)}, f32[256,8,128]{0,2,1:T(8,128)}) %tuple.61, (s32[]{:T(128)}, s32[256]{0:T(256)S(1)}, s32[]{:T(128)}, ...), branch_computations={%region_5.4_spmd, %region_6.7_spmd} | conditional | flops 275845376 | bytes 18746502 | solution.py:60
  158.3 0.5 fusion.2
  159.1 1.9 fusion.3
  161.0 1.0 copy-done.1
  162.6 4.2 %conditional.2 = ((f32[256,8]{0,1:T(8,128)S(1)}, f32[256,8]{0,1:T(8,128)S(1)}, f32[256,8,128]{0,2,1:T(8,128)})) conditional(s32[]{:T(128)} %convert_element_type.97, (f32[256,8]{0,1:T(8,128)S(1)}, f32[256,8]{0,1:T(8,128)S(1)}, f32[256,8,128]{0,2,1:T(8,128)}) %tuple.61, (s32[]{:T(128)}, s32[256]{0:T(256)S(1)}, s32[]{:T(128)}, ...), branch_computations={%region_5.4_spmd, %region_6.7_spmd} | conditional | flops 275845376 | bytes 18746502 | solution.py:60
  162.8 0.5 fusion
  163.3 0.5 fusion.2
  164.0 1.9 fusion.3
  165.9 1.0 copy-done.1
  167.6 2.4 bitcast_dynamic-update-slice_fusion.5
  170.0 0.7 dynamic-slice.2
  171.1 1.1 squeeze.35
  172.1 19.7 %while.31 = (s32[]{:T(128)}, f32[256,8]{0,1:T(8,128)S(1)}, f32[256,8]{0,1:T(8,128)S(1)}, f32[256,8,128]{0,2,1:T(8,128)}, s32[]{:T(128)}, /*index=5*/s32[256]{0:T...) while((s32[]{:T(128)}, f32[256,8]{0,1:T(8,128)S(1)}, ...), condition=%wide.region_9.9_spmd, body=%wide.region_4.8_spmd.sunk | while | flops 275845376 | bytes 18746732 | solution.py:62
  172.8 4.2 %conditional.2 = ((f32[256,8]{0,1:T(8,128)S(1)}, f32[256,8]{0,1:T(8,128)S(1)}, f32[256,8,128]{0,2,1:T(8,128)})) conditional(s32[]{:T(128)} %convert_element_type.97, (f32[256,8]{0,1:T(8,128)S(1)}, f32[256,8]{0,1:T(8,128)S(1)}, f32[256,8,128]{0,2,1:T(8,128)}) %tuple.61, (s32[]{:T(128)}, s32[256]{0:T(256)S(1)}, s32[]{:T(128)}, ...), branch_computations={%region_5.4_spmd, %region_6.7_spmd} | conditional | flops 275845376 | bytes 18746502 | solution.py:60
  173.0 0.5 fusion
  173.5 0.5 fusion.2
  174.2 1.9 fusion.3
  176.1 1.0 copy-done.1
  177.7 4.2 %conditional.2 = ((f32[256,8]{0,1:T(8,128)S(1)}, f32[256,8]{0,1:T(8,128)S(1)}, f32[256,8,128]{0,2,1:T(8,128)})) conditional(s32[]{:T(128)} %convert_element_type.97, (f32[256,8]{0,1:T(8,128)S(1)}, f32[256,8]{0,1:T(8,128)S(1)}, f32[256,8,128]{0,2,1:T(8,128)}) %tuple.61, (s32[]{:T(128)}, s32[256]{0:T(256)S(1)}, s32[]{:T(128)}, ...), branch_computations={%region_5.4_spmd, %region_6.7_spmd} | conditional | flops 275845376 | bytes 18746502 | solution.py:60
  177.9 0.5 fusion
  178.4 0.5 fusion.2
  179.1 1.9 fusion.3
  181.0 1.0 copy-done.1
  182.7 4.2 %conditional.2 = ((f32[256,8]{0,1:T(8,128)S(1)}, f32[256,8]{0,1:T(8,128)S(1)}, f32[256,8,128]{0,2,1:T(8,128)})) conditional(s32[]{:T(128)} %convert_element_type.97, (f32[256,8]{0,1:T(8,128)S(1)}, f32[256,8]{0,1:T(8,128)S(1)}, f32[256,8,128]{0,2,1:T(8,128)}) %tuple.61, (s32[]{:T(128)}, s32[256]{0:T(256)S(1)}, s32[]{:T(128)}, ...), branch_computations={%region_5.4_spmd, %region_6.7_spmd} | conditional | flops 275845376 | bytes 18746502 | solution.py:60
  182.8 0.5 fusion
  183.3 0.5 fusion.2
  184.0 1.9 fusion.3
  185.9 1.0 copy-done.1
  187.6 4.2 %conditional.2 = ((f32[256,8]{0,1:T(8,128)S(1)}, f32[256,8]{0,1:T(8,128)S(1)}, f32[256,8,128]{0,2,1:T(8,128)})) conditional(s32[]{:T(128)} %convert_element_type.97, (f32[256,8]{0,1:T(8,128)S(1)}, f32[256,8]{0,1:T(8,128)S(1)}, f32[256,8,128]{0,2,1:T(8,128)}) %tuple.61, (s32[]{:T(128)}, s32[256]{0:T(256)S(1)}, s32[]{:T(128)}, ...), branch_computations={%region_5.4_spmd, %region_6.7_spmd} | conditional | flops 275845376 | bytes 18746502 | solution.py:60
  187.7 0.5 fusion
  188.2 0.5 fusion.2
  189.0 1.9 fusion.3
  190.9 1.0 copy-done.1
  191.8 2.4 bitcast_dynamic-update-slice_fusion.5
  194.2 2.0 multiply_reduce_fusion
  196.2 7.4 %all-reduce = (f32[]{:T(128)}, f32[512]{0:T(512)S(1)}) all-reduce(f32[]{:T(128)} %convert_reduce_fusion.1, f32[512]{0:T(512)S(1)} %bitcast.86), channel_id=1, replica_groups=mesh['dp'=4,'ctx'=2,'tp'=4] {'tp'}, use_global_device_ids=true, to_apply=%region_14.15 | all-reduce | flops 513 | bytes 4104 | tf_op jit(solution)/shard_map/psum | solution.py:112
  203.6 1.9 copy.19
  206.1 9.7 %fusion.21 = bf16[512,4096]{1,0:T(8,128)(2,1)} fusion(bf16[1024,4096]{1,0:T(8,128)(2,1)} %param.15, f32[]{:T(128)S(6)} %div.44, f32[64,8,8,128]{3,2,1,0:T(8,128)} %bitcast.83, f32[1024]{0:T(1024)S(1)} %copy-done.5, f32[512]{0:T(512)S(1)} %add_rsqrt_fusion), kind=kOutput, calls=%fused_computation.38 | convolution fusion | flops 4332191744 | bytes 14686212 | tf_op jit(solution)/shard_map/dot_general | solution.py:116
  215.8 77.4 %reduce-scatter.2.cloned.1.call-done = bf16[128,4096]{1,0:T(8,128)(2,1)} async-done(((bf16[512,4096]{1,0:T(8,128)(2,1)}), bf16[128,4096]{1,0:T(8,128)(2,1)}) %reduce-scatter.2.cloned.1.call-update) | async-done | bytes 1048592 | tf_op jit(solution)/shard_map/reduce_scatter | solution.py:115
  293.2 2.4 fusion.29
  (99 shorter events, 4.1 us)
Async XLA Ops:
  6.5 86.9 %all-gather.4.cloned.1.call-start = ((), (), s32[]{:S(2)}) async-start(), calls=%async_computation.1 | async-start | bytes 5242880 | tf_op jit(solution)/shard_map/all_gather | solution.py:84
  10.6 121.7 %all-gather.6.cloned.1.call-start = ((), (), s32[]{:S(2)}) async-start(), calls=%async_computation.2 | async-start | bytes 3145728 | tf_op jit(solution)/shard_map/all_gather | solution.py:106
  117.6 28.0 %all-gather.8.cloned.1.call-start = ((), (), s32[]{:S(2)}) async-start(), calls=%async_computation.3 | async-start | bytes 3145728 | tf_op jit(solution)/shard_map/all_gather | solution.py:107
  119.0 174.2 %reduce-scatter.2.cloned.1.call-start = ((), (), s32[]{:S(2)}) async-start(), calls=%async_computation.4 | async-start | bytes 5242880 | tf_op jit(solution)/shard_map/reduce_scatter | solution.py:115
  149.9 1.0 copy-start.2
  152.9 1.2 copy-start
  156.0 1.0 copy-start.1
  157.8 1.2 copy-start
  160.9 1.0 copy-start.1
  162.8 1.2 copy-start
  165.9 1.0 copy-start.1
  167.6 2.4 copy-start.3
  170.0 1.0 copy-start.2
  173.0 1.2 copy-start
  176.1 1.0 copy-start.1
  177.9 1.2 copy-start
  181.0 1.0 copy-start.1
  182.8 1.2 copy-start
  185.9 1.0 copy-start.1
  187.7 1.2 copy-start
  190.8 1.0 copy-start.1
  191.8 2.4 copy-start.3
  203.6 2.5 copy-start.5
  215.8 77.4 %copy-start.4 = (bf16[1,128,4096]{2,1,0:T(8,128)(2,1)S(1)}, bf16[1,128,4096]{2,1,0:T(8,128)(2,1)}, u32[]{:S(2)}) copy-start(bf16[1,128,4096]{2,1,0:T(8,128)(2,1)} %param.11) | copy-start | bytes 3145732
Sparse Core Ops, SparseCore 0:
  10.7 79.7 all-gather.3
  117.7 14.5 all-gather.5
  133.9 11.7 all-gather.7
  215.9 77.2 reduce-scatter.1
where the time goes:
time: 306 us; the launch traced here: 302 us
  waiting for transfers between devices  93.2 us (30%)
  local copies, waits for them, and re-layouts  64.1 us (21%)
  other arithmetic  62.7 us (20%)
  matrix products  46.4 us (15%)
  blocking collectives  15.4 us (5%)
  between operations  13.9 us (5%)
  loops' own time  6.31 us (2%)
    reduce_scatter x1, waiting for transfers between devices, body(): lax.psum_scatter(jnp.dot(sub_normed, w_o, preferred_element_type=jnp.floa...  77.4 us
    unnamed x10, local copies, waits for them, and re-layouts  38.8 us
    convert_element_type x1, other arithmetic, quantize(): return (scale * ternary).astype(jnp.bfloat16)  25.8 us
    dot_general x1, matrix products, body(): jnp.dot(lax.all_gather(normed, 'tp', axis=0, tiled=True), w_in, preferred...  20.4 us
    reduce_sum x1, other arithmetic, body(): qkv_abs = jnp.sum(jnp.abs(w_qkv), axis=(0, 2), dtype=jnp.float32)  15.6 us
    dot_general x7, matrix products, compute(): jnp.einsum('qhk,khd->qhd', expo.astype(jnp.bfloat16), value_one, preferre...  13.1 us
    all_gather x1, waiting for transfers between devices, body(): lax.all_gather(values, 'ctx', axis=0, tiled=True)  11.2 us
    dot_general x1, matrix products, body(): jnp.dot(sub_normed, w_o, preferred_element_type=jnp.float32)  9.68 us
  transfers between devices with their start and end apart: 4, of which 3 were waited for; matrix products, arithmetic and copies ran while one was open for 29% of the time, Pallas kernels for 0%

commit v1 on v0

v1 whole, which is shorter than its diff:
```python
import functools

import jax
import jax.numpy as jnp
from jax import lax
from jax.experimental import pallas as pl
from jax.experimental.pallas import tpu as pltpu
from jax.sharding import PartitionSpec as P

HD = 128
eps_norm = 1e-05
low_value = -1e30
MESH = pl.DeviceIdType.MESH
F32 = jnp.float32
BF16 = jnp.bfloat16
VMEM_LIMIT = 60 * 1024 * 1024


def mult(x, k):
    return pl.multiple_of(x, k)


def enter(n, c, z):
    barrier = pltpu.get_barrier_semaphore()
    flat = c * n + z

    def greet(j, carry):
        other = lax.rem(flat + j, 2 * n)
        pl.semaphore_signal(
            barrier,
            inc=1,
            device_id={"ctx": other // n, "tp": lax.rem(other, n)},
            device_id_type=MESH,
        )
        return carry

    lax.fori_loop(1, 2 * n, greet, 0)
    pl.semaphore_wait(barrier, 2 * n - 1)


def tile_copy(n, c, z, src, dst, send_sem, recv_sem, j):
    flat = c * n + z
    other = lax.rem(flat + j, 2 * n)
    return pltpu.make_async_remote_copy(
        src_ref=src,
        dst_ref=dst.at[flat],
        send_sem=send_sem.at[other],
        recv_sem=recv_sem.at[flat],
        device_id={"ctx": other // n, "tp": lax.rem(other, n)},
        device_id_type=MESH,
    )


def tile_wait(n, c, z, src, dst, send_sem, recv_sem, j):
    flat = c * n + z
    other = lax.rem(flat + j, 2 * n)
    return pltpu.make_async_remote_copy(
        src_ref=src,
        dst_ref=dst.at[other],
        send_sem=send_sem.at[other],
        recv_sem=recv_sem.at[other],
        device_id={"ctx": other // n, "tp": lax.rem(other, n)},
        device_id_type=MESH,
    )


def project_kernel(
    n, count, pieces,
    x_ref, gain_ref, w_ref, wo_ref,
    qkv_ref, wo_out, scale_ref,
    held, w_held, wo_held, part, sums,
    load_sem, store_sem, tile_send, tile_recv, send_r, send_l, send_p, recv_z, recv_p,
):
    c = lax.axis_index("ctx")
    z = lax.axis_index("tp")
    rows, width = x_ref.shape
    cols = w_held.shape[2]
    deep = width // pieces
    deep_o = wo_held.shape[0] // pieces

    def load_w(m, p):
        return pltpu.make_async_copy(
            w_ref.at[m, pl.ds(p * deep, deep), pl.ds(mult(c * cols, 128), cols)],
            w_held.at[m, pl.ds(p * deep, deep)],
            load_sem.at[m * pieces + p],
        )

    def load_o(p):
        return pltpu.make_async_copy(
            wo_ref.at[pl.ds(p * deep_o, deep_o)],
            wo_held.at[pl.ds(p * deep_o, deep_o)],
            load_sem.at[3 * pieces + p],
        )

    for m in range(3):
        for p in range(pieces):
            load_w(m, p).start()
    for p in range(pieces):
        load_o(p).start()

    mine = mult(c * rows, 16)

    def norm_rows(i, carry):
        x = x_ref[pl.ds(mult(i * 16, 16), 16), :].astype(F32)
        r = lax.rsqrt(jnp.mean(x * x, axis=-1, keepdims=True) + eps_norm)
        held[z, pl.ds(mult(mine + i * 16, 16), 16), :] = (x * r * gain_ref[...]).astype(BF16)
        return carry

    lax.fori_loop(0, rows // 16, norm_rows, 0)
    enter(n, c, z)

    def move(owner, to, send_sem, recv_sem):
        block = held.at[owner, pl.ds(mine, rows)]
        return pltpu.make_async_remote_copy(
            src_ref=block,
            dst_ref=block,
            send_sem=send_sem.at[owner],
            recv_sem=recv_sem.at[owner],
            device_id=to,
            device_id_type=MESH,
        )

    def to_right(owner):
        return move(owner, {"tp": lax.rem(z + 1, n)}, send_r, recv_z)

    def to_left(owner):
        return move(owner, {"tp": lax.rem(z + n - 1, n)}, send_l, recv_z)

    def to_partner(owner):
        return move(owner, {"ctx": 1 - c}, send_p, recv_p)

    def from_partner(owner):
        block = held.at[owner, pl.ds(mult((1 - c) * rows, 16), rows)]
        return pltpu.make_async_remote_copy(
            src_ref=block,
            dst_ref=block,
            send_sem=send_p.at[owner],
            recv_sem=recv_p.at[owner],
            device_id={"ctx": 1 - c},
            device_id_type=MESH,
        )

    @pl.when(z < n - 1)
    def _():
        to_right(z).start()

    @pl.when(z > 0)
    def _():
        to_left(z).start()

    to_partner(z).start()

    part[...] = jnp.zeros_like(part)
    step_w = 32
    for m in range(3):
        total = jnp.zeros((8, cols), F32)
        for p in range(pieces):
            load_w(m, p).wait()

            def add_w(i, acc, m=m, p=p):
                at = mult(p * deep + i * step_w, step_w)
                v = jnp.abs(w_held[m, pl.ds(at, step_w), :].astype(F32))
                return acc + jnp.sum(v.reshape(step_w // 8, 8, cols), axis=0)

            total = lax.fori_loop(0, deep // step_w, add_w, total)
        one = jnp.sum(jnp.sum(total, axis=0, keepdims=True), axis=1, keepdims=True)
        part[m : m + 1, :] = jnp.broadcast_to(one, (1, 128))
    total = jnp.zeros((8, width), F32)
    for p in range(pieces):
        load_o(p).wait()

        def add_o(i, acc, p=p):
            v = jnp.abs(wo_held[pl.ds(mult(p * deep_o + i * 16, 16), 16), :].astype(F32))
            return acc + jnp.sum(v.reshape(2, 8, width), axis=0)

        total = lax.fori_loop(0, deep_o // 16, add_o, total)
    one = 0.5 * jnp.sum(jnp.sum(total, axis=0, keepdims=True), axis=1, keepdims=True)
    part[3:4, :] = jnp.broadcast_to(one, (1, 128))

    def send_tile(j, carry):
        tile_copy(n, c, z, part, sums, tile_send, tile_recv, j).start()
        return carry

    lax.fori_loop(1, 2 * n, send_tile, 0)

    def get_tile(j, acc):
        tile_wait(n, c, z, part, sums, tile_send, tile_recv, j).wait_recv()
        return acc + sums[lax.rem(c * n + z + j, 2 * n)]

    scale = lax.fori_loop(1, 2 * n, get_tile, part[...]) / count
    scale_ref[...] = scale

    def ternary(w, half):
        one = jnp.ones_like(w)
        zero = jnp.zeros_like(w)
        return jnp.where(w > half, one, jnp.where(w < -half, -one, zero))

    for m in range(3):
        half_w = jnp.broadcast_to((0.5 * scale[m : m + 1, 0:1]).astype(BF16), (step_w, cols))

        def cut_w(i, carry, m=m, half_w=half_w):
            at = pl.ds(mult(i * step_w, step_w), step_w)
            w_held[m, at, :] = ternary(w_held[m, at, :], half_w)
            return carry

        lax.fori_loop(0, width // step_w, cut_w, 0)

    block_rows = n * rows

    def compute(owner):
        from_partner(owner).wait_recv()

        def one(m, carry):
            s = scale_ref[pl.ds(m, 1), 0:1].astype(BF16).astype(F32)
            y = jnp.dot(held[owner], w_held[m], preferred_element_type=F32) * s
            y = y.astype(BF16)
            qkv_ref[m, pl.ds(mult(owner * rows, 16), rows), :] = y[:rows]
            qkv_ref[m, pl.ds(mult(block_rows + owner * rows, 16), rows), :] = y[rows:]
            return carry

        lax.fori_loop(0, 3, one, 0)

    def forward(s):
        @pl.when(z - 1 - s >= 0)
        def _():
            owner = lax.rem(z - 1 - s + n, n)
            to_right(owner).wait_recv()

            @pl.when(z < n - 1)
            def _():
                to_right(owner).start()

            to_partner(owner).start()

        @pl.when(z + 1 + s <= n - 1)
        def _():
            owner = lax.rem(z + 1 + s, n)
            to_left(owner).wait_recv()

            @pl.when(z > 0)
            def _():
                to_left(owner).start()

            to_partner(owner).start()

    def store_o():
        return pltpu.make_async_copy(wo_held, wo_out, store_sem)

    compute(z)
    half_o = jnp.broadcast_to((0.5 * scale[3:4, 0:1]).astype(BF16), (16, width))

    def cut_o(i, carry):
        at = pl.ds(mult(i * 16, 16), 16)
        wo_held[at, :] = ternary(wo_held[at, :], half_o)
        return carry

    forward(0)
    lax.fori_loop(0, wo_held.shape[0] // 16, cut_o, 0)
    store_o().start()

    def step(s, carry):
        @pl.when(s < n - 1)
        def _():
            forward(s)

        @pl.when(z - s >= 0)
        def _():
            compute(lax.rem(z - s + n, n))

        @pl.when(z + s <= n - 1)
        def _():
            compute(lax.rem(z + s, n))

        return carry

    lax.fori_loop(1, n, step, 0)

    def finish(owner, carry):
        @pl.when((owner <= z) & (z < n - 1))
        def _():
            to_right(owner).wait_send()

        @pl.when((owner >= z) & (z > 0))
        def _():
            to_left(owner).wait_send()

        to_partner(owner).wait_send()
        return carry

    lax.fori_loop(0, n, finish, 0)

    def finish_tile(j, carry):
        tile_wait(n, c, z, part, sums, tile_send, tile_recv, j).wait_send()
        return carry

    lax.fori_loop(1, 2 * n, finish_tile, 0)
    store_o().wait()


def attend_kernel(block, qkv_ref, gain_ref, out_ref, power_ref):
    rows = qkv_ref.shape[1]
    factor = (HD**-0.5) * 1.4426950408889634
    lower = lax.broadcasted_iota(jnp.int32, (block, block), 1) <= lax.broadcasted_iota(
        jnp.int32, (block, block), 0
    )
    turn = (((1,), (1,)), ((), ()))

    @pl.when(pl.program_id(0) == 0)
    def _():
        power_ref[...] = jnp.zeros_like(power_ref)

    for i in range(rows // block):
        here = slice(i * block, (i + 1) * block)
        q = qkv_ref[0, here, :]
        diag = lax.dot_general(q, qkv_ref[1, here, :], turn, preferred_element_type=F32)
        diag = jnp.where(lower, diag, low_value)
        top = jnp.max(diag, axis=-1, keepdims=True)
        if i:
            past = slice(0, i * block)
            back = lax.dot_general(q, qkv_ref[1, past, :], turn, preferred_element_type=F32)
            top = jnp.maximum(top, jnp.max(back, axis=-1, keepdims=True))
        e = jnp.exp2((diag - top) * factor)
        total = jnp.sum(e, axis=-1, keepdims=True)
        acc = jnp.dot(e.astype(BF16), qkv_ref[2, here, :], preferred_element_type=F32)
        if i:
            e = jnp.exp2((back - top) * factor)
            total = total + jnp.sum(e, axis=-1, keepdims=True)
            acc = acc + jnp.dot(e.astype(BF16), qkv_ref[2, past, :], preferred_element_type=F32)
        att = acc / total
        power_ref[here, :] += att * att
        out_ref[here, :] = (att * gain_ref[...]).astype(BF16)


def scatter_kernel(
    n, width_all,
    a_ref, power_ref, wo_ref, scale_ref, x_ref,
    out_ref,
    a_held, wo_held, mine_p, got, extra, tiles, sums,
    load_sem, keep_sem, pair_send, pair_recv, tile_send, tile_recv, send_sem, recv_sem, extra_sem,
):
    c = lax.axis_index("ctx")
    z = lax.axis_index("tp")
    rows, width = x_ref.shape
    cols = a_ref.shape[1]
    block_rows = n * rows
    load = pltpu.make_async_copy(wo_ref, wo_held, load_sem)
    load.start()
    mine = pl.ds(mult(c * block_rows, 16), block_rows)
    theirs = pl.ds(mult((1 - c) * block_rows, 16), block_rows)
    keep = pltpu.make_async_copy(a_ref.at[mine], a_held.at[c], keep_sem)
    keep.start()

    def sum_tile(b, carry):
        ones = jnp.ones((8, 128), F32)
        blk = power_ref[pl.ds(mult(b * rows, 8), rows), :]
        tiles[b] = lax.dot_general(
            ones, blk, (((1,), (1,)), ((), ())),
            precision=lax.Precision.HIGHEST, preferred_element_type=F32,
        )
        return carry

    lax.fori_loop(0, 2 * n, sum_tile, 0)
    enter(n, c, z)
    swap = pltpu.make_async_remote_copy(
        src_ref=a_ref.at[theirs],
        dst_ref=a_held.at[c],
        send_sem=pair_send,
        recv_sem=pair_recv,
        device_id={"ctx": 1 - c},
        device_id_type=MESH,
    )
    swap.start()

    def send_tile(j, carry):
        other = lax.rem(c * n + z + j, 2 * n)
        tile_copy(n, c, z, tiles.at[other], sums, tile_send, tile_recv, j).start()
        return carry

    lax.fori_loop(1, 2 * n, send_tile, 0)
    keep.wait()
    load.wait()
    swap.wait_recv()

    left = {"tp": lax.rem(z + n - 1, n)}
    right = {"tp": lax.rem(z + 1, n)}

    def move(t, dst, recv, to):
        return pltpu.make_async_remote_copy(
            src_ref=mine_p.at[t],
            dst_ref=dst,
            send_sem=send_sem.at[t],
            recv_sem=recv,
            device_id=to,
            device_id_type=MESH,
        )

    def to_left(t):
        return move(t, got.at[t], recv_sem.at[t], left)

    def to_right_pass(t):
        return move(t, got.at[t], recv_sem.at[t], right)

    def to_right_last(t):
        return move(t, extra, extra_sem, right)

    def start_right(t):
        @pl.when(t == z + 1)
        def _():
            to_right_last(t).start()

        @pl.when(t > z + 1)
        def _():
            to_right_pass(t).start()

    tn = min(512, width)
    scale_o = scale_ref[3:4, 0:1].astype(BF16).astype(F32)

    def target(i):
        return lax.select(2 * z >= n, i, n - 1 - i)

    def first(i, carry):
        t = target(i)
        at = pl.ds(mult(t * rows, 16), rows)

        def cols_of(k, inner):
            there = pl.ds(mult(k * tn, 128), tn)
            y = jnp.dot(a_held[0, at, :], wo_held[:cols, there], preferred_element_type=F32)
            y = y + jnp.dot(a_held[1, at, :], wo_held[cols:, there], preferred_element_type=F32)
            mine_p[t, :, there] = (y * scale_o).astype(BF16)
            return inner

        lax.fori_loop(0, width // tn, cols_of, 0)

        @pl.when((z == n - 1) & (t < z))
        def _():
            to_left(t).start()

        @pl.when((z == 0) & (t > z))
        def _():
            start_right(t)

        return carry

    lax.fori_loop(0, n, first, 0)

    def add_got(t):
        def some(i, inner):
            at = pl.ds(mult(i * 16, 16), 16)
            mine_p[t, at, :] = (
                mine_p[t, at, :].astype(F32) + got[t, at, :].astype(F32)
            ).astype(BF16)
            return inner

        lax.fori_loop(0, rows // 16, some, 0)

    def pass_left(t):
        @pl.when((t < z) & (z < n - 1))
        def _():
            to_left(t).wait_recv()
            add_got(t)
            to_left(t).start()

    def pass_right(t):
        @pl.when((t > z) & (z > 0))
        def _():
            to_right_pass(t).wait_recv()
            add_got(t)
            start_right(t)

    def second(i, carry):
        @pl.when(2 * z >= n)
        def _():
            pass_left(i)

        pass_right(n - 1 - i)

        @pl.when(2 * z < n)
        def _():
            pass_left(i)

        return carry

    lax.fori_loop(0, n, second, 0)

    def get_tile(j, acc):
        tile_wait(n, c, z, tiles.at[0], sums, tile_send, tile_recv, j).wait_recv()
        return acc + sums[lax.rem(c * n + z + j, 2 * n)]

    power = lax.fori_loop(1, 2 * n, get_tile, tiles[c * n + z]) / width_all
    r = lax.rsqrt(power[0:1, :] + eps_norm)
    r_col = jnp.transpose(jnp.broadcast_to(r, (rows, rows)))
    tiles_of = width // rows
    sums_r = r_col

    @pl.when(z < n - 1)
    def _():
        to_left(z).wait_recv()

    @pl.when(z > 0)
    def _():
        to_right_last(z).wait_recv()

    @pl.when(z == n - 1)
    def _():
        got[z] = jnp.zeros((rows, width), BF16)

    @pl.when(z == 0)
    def _():
        extra[...] = jnp.zeros((rows, width), BF16)

    def last(k, carry):
        at = pl.ds(mult(k * rows, 128), rows)
        y = mine_p[z, :, at].astype(F32) + got[z, :, at].astype(F32) + extra[:, at].astype(F32)
        out_ref[:, at] = (x_ref[:, at].astype(F32) + y * sums_r).astype(BF16)
        return carry

    lax.fori_loop(0, tiles_of, last, 0)

    def finish(t, carry):
        @pl.when(t < z)
        def _():
            to_left(t).wait_send()

        @pl.when(t > z)
        def _():
            to_right_pass(t).wait_send()

        return carry

    lax.fori_loop(0, n, finish, 0)

    def finish_tile(j, carry):
        tile_wait(n, c, z, tiles.at[0], sums, tile_send, tile_recv, j).wait_send()
        return carry

    lax.fori_loop(1, 2 * n, finish_tile, 0)
    swap.wait_send()


def body(n, tokens, norm_gain, w_qkv, sub_gain, w_out):
    x = tokens[0]
    rows, width = x.shape
    head_cols = w_qkv.shape[2]
    cols = head_cols // 2
    heads = cols // HD
    all_rows = 2 * n * rows
    count = float(width * n * head_cols)
    pieces = 4
    w = jnp.transpose(w_qkv, (1, 0, 2))
    dma = pltpu.SemaphoreType.DMA
    vm = pl.BlockSpec(memory_space=pltpu.VMEM)
    hbm = pl.BlockSpec(memory_space=pl.ANY)
    qkv, wo, scale = pl.pallas_call(
        functools.partial(project_kernel, n, count, pieces),
        out_shape=(
            jax.ShapeDtypeStruct((3, all_rows, cols), BF16),
            jax.ShapeDtypeStruct(w_out.shape, BF16),
            jax.ShapeDtypeStruct((8, 128), F32),
        ),
        in_specs=[vm, vm, hbm, hbm],
        out_specs=(vm, hbm, vm),
        scratch_shapes=[
            pltpu.VMEM((n, 2 * rows, width), BF16),
            pltpu.VMEM((3, width, cols), BF16),
            pltpu.VMEM(w_out.shape, BF16),
            pltpu.VMEM((8, 128), F32),
            pltpu.VMEM((2 * n, 8, 128), F32),
            dma((4 * pieces,)),
            dma(()),
            dma((2 * n,)),
            dma((2 * n,)),
            dma((n,)),
            dma((n,)),
            dma((n,)),
            dma((n,)),
            dma((n,)),
        ],
        compiler_params=pltpu.CompilerParams(
            collective_id=0, has_side_effects=True, vmem_limit_bytes=VMEM_LIMIT
        ),
        name="project",
    )(x, norm_gain.reshape(1, width), w, w_out)

    gain = lax.dynamic_slice(sub_gain, (lax.axis_index("ctx") * cols,), (cols,)).reshape(1, cols)
    att, power = pl.pallas_call(
        functools.partial(attend_kernel, 256),
        grid=(heads,),
        out_shape=(
            jax.ShapeDtypeStruct((all_rows, cols), BF16),
            jax.ShapeDtypeStruct((all_rows, HD), F32),
        ),
        in_specs=[
            pl.BlockSpec((3, all_rows, HD), lambda h: (0, 0, h)),
            pl.BlockSpec((1, HD), lambda h: (0, h)),
        ],
        out_specs=(
            pl.BlockSpec((all_rows, HD), lambda h: (0, h)),
            pl.BlockSpec((all_rows, HD), lambda h: (0, 0)),
        ),
        compiler_params=pltpu.CompilerParams(
            dimension_semantics=("arbitrary",), vmem_limit_bytes=VMEM_LIMIT
        ),
        name="attend",
    )(qkv, gain)

    out = pl.pallas_call(
        functools.partial(scatter_kernel, n, float(n * head_cols)),
        out_shape=jax.ShapeDtypeStruct((rows, width), BF16),
        in_specs=[vm, vm, hbm, vm, vm],
        out_specs=vm,
        scratch_shapes=[
            pltpu.VMEM((2, n * rows, cols), BF16),
            pltpu.VMEM(w_out.shape, BF16),
            pltpu.VMEM((n, rows, width), BF16),
            pltpu.VMEM((n, rows, width), BF16),
            pltpu.VMEM((rows, width), BF16),
            pltpu.VMEM((2 * n, 8, 128), F32),
            pltpu.VMEM((2 * n, 8, 128), F32),
            dma(()),
            dma(()),
            dma(()),
            dma(()),
            dma((2 * n,)),
            dma((2 * n,)),
            dma((n,)),
            dma((n,)),
            dma(()),
        ],
        compiler_params=pltpu.CompilerParams(
            collective_id=1, has_side_effects=True, vmem_limit_bytes=VMEM_LIMIT
        ),
        name="scatter",
    )(att, power, wo, scale, x)
    return out[None]


def solution(mesh):
    return jax.shard_map(
        functools.partial(body, mesh.shape["tp"]),
        mesh=mesh,
        in_specs=(P("dp", ("ctx", "tp"), None), P(), P(None, None, "tp"), P("tp"), P("tp", None)),
        out_specs=P("dp", ("ctx", "tp"), None),
        check_vma=False,
    )
```

time: 306 us -> 197 us (0.64)
  Pallas kernels: 0 us -> 189 us
  waiting for transfers between devices: 93.2 us -> 0 us
  other arithmetic: 62.7 us -> 0 us
  local copies, waits for them, and re-layouts: 64.1 us -> 3.64 us
  matrix products: 46.4 us -> 0 us
  blocking collectives: 15.4 us -> 0 us
  between operations: 13.9 us -> 0.02 us
  loops' own time: 6.31 us -> 0 us
    pallas_call x0 -> x3, Pallas kernels: none -> 189 us  [the longest x1 93.4 us: body(): pl.pallas_call(functools.partial(scatter_kernel, n, float(n * head_cols))...]
    reduce_scatter x1 -> x0, waiting for transfers between devices: 77.4 us -> none  [body(): lax.psum_scatter(jnp.dot(sub_normed, w_o, preferred_element_type=jnp.floa...]
    dot_general x16 -> x0, matrix products: 46.4 us -> none  [the longest x1 20.4 us: body(): jnp.dot(lax.all_gather(normed, 'tp', axis=0, tiled=True), w_in, preferred...]
    unnamed x10 -> x1, local copies, waits for them, and re-layouts: 38.8 us -> 2.29 us
    reduce_sum x11 -> x0, other arithmetic: 31 us -> none  [the longest x1 15.6 us: body(): qkv_abs = jnp.sum(jnp.abs(w_qkv), axis=(0, 2), dtype=jnp.float32)]
    convert_element_type x2 -> x0, other arithmetic: 28.3 us -> none  [the longest x1 25.8 us: quantize(): return (scale * ternary).astype(jnp.bfloat16)]
    all_gather x3 -> x0, waiting for transfers between devices: 15.7 us -> none  [the longest x1 11.2 us: body(): lax.all_gather(values, 'ctx', axis=0, tiled=True)]
    psum x2 -> x0, blocking collectives: 15.4 us -> none  [the longest x1 7.97 us: body(): qkv_total = lax.psum(qkv_abs, 'tp')]
  transfers between devices with their start and end apart: 4 -> 0, of which waited for: 3 -> 0; matrix products, arithmetic and copies ran while one was open for 29% -> 0% of each run, Pallas kernels for 0% -> 0%
where the time goes in v1:
time: 197 us; the launch traced here: 193 us
  Pallas kernels  189 us (96%)
  local copies, waits for them, and re-layouts  3.64 us (2%)
    pallas_call x1, Pallas kernels, body(): pl.pallas_call(functools.partial(scatter_kernel, n, float(n * head_cols))...  93.4 us
    pallas_call x1, Pallas kernels, body(): pl.pallas_call(functools.partial(project_kernel, n, count, pieces), out_s...  86.8 us
    pallas_call x1, Pallas kernels, body(): pl.pallas_call(functools.partial(attend_kernel, 256), grid=(heads,), out_...  9.01 us

profile of v1, /device:TPU:15, one launch (start us, length us, event | category | flops | bytes accessed | tf_op | source)
XLA Modules:
  0.0 192.8 jit_solution(17850551219943341582)
XLA Ops:
  0.0 1.3 dynamic_slice.3
  1.3 86.8 %project.1 = (bf16[3,1024,512]{2,1,0:T(8,128)(2,1)}, bf16[1024,4096]{1,0:T(8,128)(2,1)}, f32[8,128]{1,0:T(8,128)}) custom-call(bf16[128,4096]{1,0:T(8,128)(2,1)} %bitcast.6, f32[1,4096]{1,0:T(1,128)} %bitcast.9, bf16[3,4096,1024]{2,1,0:T(8,128)(2,1)} %bitcast.5, bf16[1024,4096]{1,0:T(8,128)(2,1)} %wo_ref.1), custom_call_target="tpu_custom_call" | custom-call | tf_op jit(solution)/shard_map/project/pallas_call | solution.py:553
  88.2 9.0 %attend.1 = (bf16[1024,512]{1,0:T(8,128)(2,1)}, f32[1024,128]{1,0:T(8,128)}) custom-call(bf16[3,1024,512]{2,1,0:T(8,128)(2,1)} %get-tuple-element.10.qkv_ref, f32[1,512]{1,0:T(1,128)} %bitcast.10), custom_call_target="tpu_custom_call" | custom-call | tf_op jit(solution)/shard_map/attend/pallas_call | solution.py:585
  97.2 93.4 %scatter.1 = bf16[128,4096]{1,0:T(8,128)(2,1)} custom-call(bf16[1024,512]{1,0:T(8,128)(2,1)} %get-tuple-element.11.a_ref, f32[1024,128]{1,0:T(8,128)} %get-tuple-element.12.power_ref, bf16[1024,4096]{1,0:T(8,128)(2,1)} %get-tuple-element.13.wo_ref, f32[8,128]{1,0:T(8,128)} %get-tuple-element.14.scale_ref, bf16[128,4096]{1,0:T(8,128)(2,1)} %bitcast.7), custom_call_target="tpu_custom_call" | custom-call | tf_op jit(solution)/shard_map/scatter/pallas_call | solution.py:606
  190.5 2.3 %copy.7 = bf16[1,128,4096]{2,1,0:T(8,128)(2,1)} copy(bf16[1,128,4096]{2,1,0:T(8,128)(2,1)} %bitcast.8) | data formatting | bytes 2097152

commit v2 on v1

--- a/solution.py
+++ b/solution.py
@@ -64,12 +64,15 @@
     )
 
 
-def project_kernel(
-    n, count, pieces,
-    x_ref, gain_ref, w_ref, wo_ref,
-    qkv_ref, wo_out, scale_ref,
-    held, w_held, wo_held, part, sums,
-    load_sem, store_sem, tile_send, tile_recv, send_r, send_l, send_p, recv_z, recv_p,
+def layer_kernel(
+    n, count, width_all, pieces, block,
+    x_ref, gain_ref, w_ref, sub_ref, wo_ref,
+    out_ref,
+    held, w_held, wo_held, qkv_ref, scale_ref, part, sums,
+    a_ref, a_held, power_ref, extra, tiles, psums,
+    load_sem, tile_send, tile_recv, send_r, send_l, send_p, recv_z, recv_p,
+    free_l, free_r, keep_sem, pair_send, pair_recv, ptile_send, ptile_recv,
+    send_sem, recv_sem, extra_sem,
 ):
     c = lax.axis_index("ctx")
     z = lax.axis_index("tp")
@@ -183,6 +186,31 @@
 
     lax.fori_loop(1, 2 * n, send_tile, 0)
 
+    def forward(s):
+        @pl.when(z - 1 - s >= 0)
+        def _():
+            owner = lax.rem(z - 1 - s + n, n)
+            to_right(owner).wait_recv()
+
+            @pl.when(z < n - 1)
+            def _():
+                to_right(owner).start()
+
+            to_partner(owner).start()
+
+        @pl.when(z + 1 + s <= n - 1)
+        def _():
+            owner = lax.rem(z + 1 + s, n)
+            to_left(owner).wait_recv()
+
+            @pl.when(z > 0)
+            def _():
+                to_left(owner).start()
+
+            to_partner(owner).start()
+
+    forward(0)
+
     def get_tile(j, acc):
         tile_wait(n, c, z, part, sums, tile_send, tile_recv, j).wait_recv()
         return acc + sums[lax.rem(c * n + z + j, 2 * n)]
@@ -220,60 +248,42 @@
 
         lax.fori_loop(0, 3, one, 0)
 
-    def forward(s):
+    compute(z)
+
+    def cut_out():
+        half_o = jnp.broadcast_to((0.5 * scale_ref[3:4, 0:1]).astype(BF16), (16, width))
+
+        def cut_o(i, carry):
+            at = pl.ds(mult(i * 16, 16), 16)
+            wo_held[at, :] = ternary(wo_held[at, :], half_o)
+            return carry
+
+        lax.fori_loop(0, wo_held.shape[0] // 16, cut_o, 0)
+
+    def compute_both(s):
         @pl.when(z - 1 - s >= 0)
         def _():
-            owner = lax.rem(z - 1 - s + n, n)
-            to_right(owner).wait_recv()
-
-            @pl.when(z < n - 1)
-            def _():
-                to_right(owner).start()
-
-            to_partner(owner).start()
+            compute(lax.rem(z - 1 - s + n, n))
 
         @pl.when(z + 1 + s <= n - 1)
         def _():
-            owner = lax.rem(z + 1 + s, n)
-            to_left(owner).wait_recv()
-
-            @pl.when(z > 0)
-            def _():
-                to_left(owner).start()
-
-            to_partner(owner).start()
-
-    def store_o():
-        return pltpu.make_async_copy(wo_held, wo_out, store_sem)
-
-    compute(z)
-    half_o = jnp.broadcast_to((0.5 * scale[3:4, 0:1]).astype(BF16), (16, width))
-
-    def cut_o(i, carry):
-        at = pl.ds(mult(i * 16, 16), 16)
-        wo_held[at, :] = ternary(wo_held[at, :], half_o)
-        return carry
-
-    forward(0)
-    lax.fori_loop(0, wo_held.shape[0] // 16, cut_o, 0)
-    store_o().start()
+            compute(lax.rem(z + 1 + s, n))
+
+    compute_both(0)
+    if n < 3:
+        cut_out()
 
     def step(s, carry):
-        @pl.when(s < n - 1)
-        def _():
-            forward(s)
-
-        @pl.when(z - s >= 0)
-        def _():
-            compute(lax.rem(z - s + n, n))
-
-        @pl.when(z + s <= n - 1)
-        def _():
-            compute(lax.rem(z + s, n))
-
-        return carry
-
-    lax.fori_loop(1, n, step, 0)
+        forward(s)
+        compute_both(s)
+
+        @pl.when(s == 1)
+        def _():
+            cut_out()
+
+        return carry
+
+    lax.fori_loop(1, n - 1, step, 0)
 
     def finish(owner, carry):
         @pl.when((owner <= z) & (z < n - 1))
@@ -289,66 +299,106 @@
 
     lax.fori_loop(0, n, finish, 0)
 
-    def finish_tile(j, carry):
-        tile_wait(n, c, z, part, sums, tile_send, tile_recv, j).wait_send()
-        return carry
-
-    lax.fori_loop(1, 2 * n, finish_tile, 0)
-    store_o().wait()
-
-
-def attend_kernel(block, qkv_ref, gain_ref, out_ref, power_ref):
-    rows = qkv_ref.shape[1]
+    @pl.when(z > 0)
+    def _():
+        pl.semaphore_signal(free_r, inc=1, device_id={"tp": lax.rem(z + n - 1, n)}, device_id_type=MESH)
+
+    @pl.when(z < n - 1)
+    def _():
+        pl.semaphore_signal(free_l, inc=1, device_id={"tp": lax.rem(z + 1, n)}, device_id_type=MESH)
+
+    mine_rows = pl.ds(mult(c * block_rows, 16), block_rows)
+    their_rows = pl.ds(mult((1 - c) * block_rows, 16), block_rows)
+
+    def swap(h):
+        at = pl.ds(mult(h * HD, 128), HD)
+        return pltpu.make_async_remote_copy(
+            src_ref=a_ref.at[their_rows, at],
+            dst_ref=a_held.at[c, :, at],
+            send_sem=pair_send.at[h],
+            recv_sem=pair_recv.at[h],
+            device_id={"ctx": 1 - c},
+            device_id_type=MESH,
+        )
+
+    def keep(h):
+        at = pl.ds(mult(h * HD, 128), HD)
+        return pltpu.make_async_copy(a_ref.at[mine_rows, at], a_held.at[c, :, at], keep_sem.at[h])
+
     factor = (HD**-0.5) * 1.4426950408889634
     lower = lax.broadcasted_iota(jnp.int32, (block, block), 1) <= lax.broadcasted_iota(
         jnp.int32, (block, block), 0
     )
     turn = (((1,), (1,)), ((), ()))
-
-    @pl.when(pl.program_id(0) == 0)
-    def _():
-        power_ref[...] = jnp.zeros_like(power_ref)
-
-    for i in range(rows // block):
-        here = slice(i * block, (i + 1) * block)
-        q = qkv_ref[0, here, :]
-        diag = lax.dot_general(q, qkv_ref[1, here, :], turn, preferred_element_type=F32)
-        diag = jnp.where(lower, diag, low_value)
-        top = jnp.max(diag, axis=-1, keepdims=True)
-        if i:
+    power_ref[...] = jnp.zeros_like(power_ref)
+
+    def head(h, carry):
+        at = pl.ds(mult(h * HD, 128), HD)
+        gain = sub_ref[:, pl.ds(mult(c * cols + h * HD, 128), HD)]
+        def finish_rows(here, acc, total):
+            att = acc / total
+            power_ref[here, :] += att * att
+            a_ref[here, at] = (att * gain).astype(BF16)
+
+        def diagonal(here):
+            q = qkv_ref[0, here, at]
+            diag = lax.dot_general(q, qkv_ref[1, here, at], turn, preferred_element_type=F32)
+            return q, jnp.where(lower, diag, low_value)
+
+        def whole_rows(i):
+            here = slice(i * block, (i + 1) * block)
             past = slice(0, i * block)
-            back = lax.dot_general(q, qkv_ref[1, past, :], turn, preferred_element_type=F32)
-            top = jnp.maximum(top, jnp.max(back, axis=-1, keepdims=True))
-        e = jnp.exp2((diag - top) * factor)
-        total = jnp.sum(e, axis=-1, keepdims=True)
-        acc = jnp.dot(e.astype(BF16), qkv_ref[2, here, :], preferred_element_type=F32)
-        if i:
-            e = jnp.exp2((back - top) * factor)
-            total = total + jnp.sum(e, axis=-1, keepdims=True)
-            acc = acc + jnp.dot(e.astype(BF16), qkv_ref[2, past, :], preferred_element_type=F32)
-        att = acc / total
-        power_ref[here, :] += att * att
-        out_ref[here, :] = (att * gain_ref[...]).astype(BF16)
-
-
-def scatter_kernel(
-    n, width_all,
-    a_ref, power_ref, wo_ref, scale_ref, x_ref,
-    out_ref,
-    a_held, wo_held, mine_p, got, extra, tiles, sums,
-    load_sem, keep_sem, pair_send, pair_recv, tile_send, tile_recv, send_sem, recv_sem, extra_sem,
-):
-    c = lax.axis_index("ctx")
-    z = lax.axis_index("tp")
-    rows, width = x_ref.shape
-    cols = a_ref.shape[1]
-    block_rows = n * rows
-    load = pltpu.make_async_copy(wo_ref, wo_held, load_sem)
-    load.start()
-    mine = pl.ds(mult(c * block_rows, 16), block_rows)
-    theirs = pl.ds(mult((1 - c) * block_rows, 16), block_rows)
-    keep = pltpu.make_async_copy(a_ref.at[mine], a_held.at[c], keep_sem)
-    keep.start()
+            q, diag = diagonal(here)
+            top = jnp.max(diag, axis=-1, keepdims=True)
+            if i:
+                back = lax.dot_general(q, qkv_ref[1, past, at], turn, preferred_element_type=F32)
+                top = jnp.maximum(top, jnp.max(back, axis=-1, keepdims=True))
+            e = jnp.exp2((diag - top) * factor)
+            total = jnp.sum(e, axis=-1, keepdims=True)
+            acc = jnp.dot(e.astype(BF16), qkv_ref[2, here, at], preferred_element_type=F32)
+            if i:
+                e = jnp.exp2((back - top) * factor)
+                total = total + jnp.sum(e, axis=-1, keepdims=True)
+                acc = acc + jnp.dot(e.astype(BF16), qkv_ref[2, past, at], preferred_element_type=F32)
+            finish_rows(here, acc, total)
+
+        def running_rows(i, carry):
+            here = pl.ds(mult(i * block, block), block)
+            q, diag = diagonal(here)
+            top = jnp.max(diag, axis=-1, keepdims=True)
+            e = jnp.exp2((diag - top) * factor)
+            total = jnp.sum(e, axis=-1, keepdims=True)
+            acc = jnp.dot(e.astype(BF16), qkv_ref[2, here, at], preferred_element_type=F32)
+
+            def back_tile(j, state):
+                top, total, acc = state
+                past = pl.ds(mult(j * block, block), block)
+                back = lax.dot_general(q, qkv_ref[1, past, at], turn, preferred_element_type=F32)
+                top_new = jnp.maximum(top, jnp.max(back, axis=-1, keepdims=True))
+                e = jnp.exp2((back - top_new) * factor)
+                old = jnp.exp2((top - top_new) * factor)
+                total = total * old + jnp.sum(e, axis=-1, keepdims=True)
+                acc = acc * old + jnp.dot(
+                    e.astype(BF16), qkv_ref[2, past, at], preferred_element_type=F32
+                )
+                return top_new, total, acc
+
+            top, total, acc = lax.fori_loop(0, i, back_tile, (top, total, acc))
+            finish_rows(here, acc, total)
+            return carry
+
+        q_count = 2 * block_rows // block
+        if q_count <= 4:
+            for i in range(q_count):
+                whole_rows(i)
+        else:
+            lax.fori_loop(0, q_count, running_rows, 0)
+        swap(h).start()
+        keep(h).start()
+        return carry
+
+    heads = cols // HD
+    lax.fori_loop(0, heads, head, 0)
 
     def sum_tile(b, carry):
         ones = jnp.ones((8, 128), F32)
@@ -360,33 +410,37 @@
         return carry
 
     lax.fori_loop(0, 2 * n, sum_tile, 0)
-    enter(n, c, z)
-    swap = pltpu.make_async_remote_copy(
-        src_ref=a_ref.at[theirs],
-        dst_ref=a_held.at[c],
-        send_sem=pair_send,
-        recv_sem=pair_recv,
-        device_id={"ctx": 1 - c},
-        device_id_type=MESH,
-    )
-    swap.start()
-
-    def send_tile(j, carry):
+    def send_power(j, carry):
         other = lax.rem(c * n + z + j, 2 * n)
-        tile_copy(n, c, z, tiles.at[other], sums, tile_send, tile_recv, j).start()
-        return carry
-
-    lax.fori_loop(1, 2 * n, send_tile, 0)
-    keep.wait()
-    load.wait()
-    swap.wait_recv()
+        tile_copy(n, c, z, tiles.at[other], psums, ptile_send, ptile_recv, j).start()
+        return carry
+
+    lax.fori_loop(1, 2 * n, send_power, 0)
+
+    def arrived(h, carry):
+        keep(h).wait()
+        swap(h).wait_recv()
+        return carry
+
+    lax.fori_loop(0, heads, arrived, 0)
+
+    @pl.when(z > 0)
+    def _():
+        pl.semaphore_wait(free_l, 1)
+
+    @pl.when(z < n - 1)
+    def _():
+        pl.semaphore_wait(free_r, 1)
+
+    sum_at = pl.ds(0, rows)
+    got_at = pl.ds(rows, rows)
 
     left = {"tp": lax.rem(z + n - 1, n)}
     right = {"tp": lax.rem(z + 1, n)}
 
-    def move(t, dst, recv, to):
+    def move_sum(t, dst, recv, to):
         return pltpu.make_async_remote_copy(
-            src_ref=mine_p.at[t],
+            src_ref=held.at[t, sum_at],
             dst_ref=dst,
             send_sem=send_sem.at[t],
             recv_sem=recv,
@@ -394,14 +448,14 @@
             device_id_type=MESH,
         )
 
-    def to_left(t):
-        return move(t, got.at[t], recv_sem.at[t], left)
+    def sum_left(t):
+        return move_sum(t, held.at[t, got_at], recv_sem.at[t], left)
 
     def to_right_pass(t):
-        return move(t, got.at[t], recv_sem.at[t], right)
+        return move_sum(t, held.at[t, got_at], recv_sem.at[t], right)
 
     def to_right_last(t):
-        return move(t, extra, extra_sem, right)
+        return move_sum(t, extra, extra_sem, right)
 
     def start_right(t):
         @pl.when(t == z + 1)
@@ -426,14 +480,14 @@
             there = pl.ds(mult(k * tn, 128), tn)
             y = jnp.dot(a_held[0, at, :], wo_held[:cols, there], preferred_element_type=F32)
             y = y + jnp.dot(a_held[1, at, :], wo_held[cols:, there], preferred_element_type=F32)
-            mine_p[t, :, there] = (y * scale_o).astype(BF16)
+            held[t, sum_at, there] = (y * scale_o).astype(BF16)
             return inner
 
         lax.fori_loop(0, width // tn, cols_of, 0)
 
         @pl.when((z == n - 1) & (t < z))
         def _():
-            to_left(t).start()
+            sum_left(t).start()
 
         @pl.when((z == 0) & (t > z))
         def _():
@@ -446,8 +500,9 @@
     def add_got(t):
         def some(i, inner):
             at = pl.ds(mult(i * 16, 16), 16)
-            mine_p[t, at, :] = (
-                mine_p[t, at, :].astype(F32) + got[t, at, :].astype(F32)
+            there = pl.ds(mult(rows + i * 16, 16), 16)
+            held[t, at, :] = (
+                held[t, at, :].astype(F32) + held[t, there, :].astype(F32)
             ).astype(BF16)
             return inner
 
@@ -456,9 +511,9 @@
     def pass_left(t):
         @pl.when((t < z) & (z < n - 1))
         def _():
-            to_left(t).wait_recv()
+            sum_left(t).wait_recv()
             add_got(t)
-            to_left(t).start()
+            sum_left(t).start()
 
     def pass_right(t):
         @pl.when((t > z) & (z > 0))
@@ -483,8 +538,8 @@
     lax.fori_loop(0, n, second, 0)
 
     def get_tile(j, acc):
-        tile_wait(n, c, z, tiles.at[0], sums, tile_send, tile_recv, j).wait_recv()
-        return acc + sums[lax.rem(c * n + z + j, 2 * n)]
+        tile_wait(n, c, z, tiles.at[0], psums, ptile_send, ptile_recv, j).wait_recv()
+        return acc + psums[lax.rem(c * n + z + j, 2 * n)]
 
     power = lax.fori_loop(1, 2 * n, get_tile, tiles[c * n + z]) / width_all
     r = lax.rsqrt(power[0:1, :] + eps_norm)
@@ -494,7 +549,7 @@
 
     @pl.when(z < n - 1)
     def _():
-        to_left(z).wait_recv()
+        sum_left(z).wait_recv()
 
     @pl.when(z > 0)
     def _():
@@ -502,7 +557,7 @@
 
     @pl.when(z == n - 1)
     def _():
-        got[z] = jnp.zeros((rows, width), BF16)
+        held[z, got_at, :] = jnp.zeros((rows, width), BF16)
 
     @pl.when(z == 0)
     def _():
@@ -510,16 +565,16 @@
 
     def last(k, carry):
         at = pl.ds(mult(k * rows, 128), rows)
-        y = mine_p[z, :, at].astype(F32) + got[z, :, at].astype(F32) + extra[:, at].astype(F32)
+        y = held[z, sum_at, at].astype(F32) + held[z, got_at, at].astype(F32) + extra[:, at].astype(F32)
         out_ref[:, at] = (x_ref[:, at].astype(F32) + y * sums_r).astype(BF16)
         return carry
 
     lax.fori_loop(0, tiles_of, last, 0)
 
-    def finish(t, carry):
+    def finish_sum(t, carry):
         @pl.when(t < z)
         def _():
-            to_left(t).wait_send()
+            sum_left(t).wait_send()
 
         @pl.when(t > z)
         def _():
@@ -527,14 +582,20 @@
 
         return carry
 
-    lax.fori_loop(0, n, finish, 0)
+    lax.fori_loop(0, n, finish_sum, 0)
 
     def finish_tile(j, carry):
-        tile_wait(n, c, z, tiles.at[0], sums, tile_send, tile_recv, j).wait_send()
+        tile_wait(n, c, z, part, sums, tile_send, tile_recv, j).wait_send()
+        tile_wait(n, c, z, tiles.at[0], psums, ptile_send, ptile_recv, j).wait_send()
         return carry
 
     lax.fori_loop(1, 2 * n, finish_tile, 0)
-    swap.wait_send()
+
+    def finish_pair(h, carry):
+        swap(h).wait_send()
+        return carry
+
+    lax.fori_loop(0, heads, finish_pair, 0)
 
 
 def body(n, tokens, norm_gain, w_qkv, sub_gain, w_out):
@@ -548,25 +609,29 @@
     pieces = 4
     w = jnp.transpose(w_qkv, (1, 0, 2))
     dma = pltpu.SemaphoreType.DMA
+    regular = pltpu.SemaphoreType.REGULAR
     vm = pl.BlockSpec(memory_space=pltpu.VMEM)
     hbm = pl.BlockSpec(memory_space=pl.ANY)
-    qkv, wo, scale = pl.pallas_call(
-        functools.partial(project_kernel, n, count, pieces),
-        out_shape=(
-            jax.ShapeDtypeStruct((3, all_rows, cols), BF16),
-            jax.ShapeDtypeStruct(w_out.shape, BF16),
-            jax.ShapeDtypeStruct((8, 128), F32),
-        ),
-        in_specs=[vm, vm, hbm, hbm],
-        out_specs=(vm, hbm, vm),
+    out = pl.pallas_call(
+        functools.partial(layer_kernel, n, count, float(n * head_cols), pieces, 256),
+        out_shape=jax.ShapeDtypeStruct((rows, width), BF16),
+        in_specs=[vm, vm, hbm, vm, hbm],
+        out_specs=vm,
         scratch_shapes=[
             pltpu.VMEM((n, 2 * rows, width), BF16),
             pltpu.VMEM((3, width, cols), BF16),
             pltpu.VMEM(w_out.shape, BF16),
+            pltpu.VMEM((3, all_rows, cols), BF16),
+            pltpu.VMEM((8, 128), F32),
             pltpu.VMEM((8, 128), F32),
             pltpu.VMEM((2 * n, 8, 128), F32),
+            pltpu.VMEM((all_rows, cols), BF16),
+            pltpu.VMEM((2, n * rows, cols), BF16),
+            pltpu.VMEM((all_rows, HD), F32),
+            pltpu.VMEM((rows, width), BF16),
+            pltpu.VMEM((2 * n, 8, 128), F32),
+            pltpu.VMEM((2 * n, 8, 128), F32),
             dma((4 * pieces,)),
-            dma(()),
             dma((2 * n,)),
             dma((2 * n,)),
             dma((n,)),
@@ -574,52 +639,11 @@
             dma((n,)),
             dma((n,)),
             dma((n,)),
-        ],
-        compiler_params=pltpu.CompilerParams(
-            collective_id=0, has_side_effects=True, vmem_limit_bytes=VMEM_LIMIT
-        ),
-        name="project",
-    )(x, norm_gain.reshape(1, width), w, w_out)
-
-    gain = lax.dynamic_slice(sub_gain, (lax.axis_index("ctx") * cols,), (cols,)).reshape(1, cols)
-    att, power = pl.pallas_call(
-        functools.partial(attend_kernel, 256),
-        grid=(heads,),
-        out_shape=(
-            jax.ShapeDtypeStruct((all_rows, cols), BF16),
-            jax.ShapeDtypeStruct((all_rows, HD), F32),
-        ),
-        in_specs=[
-            pl.BlockSpec((3, all_rows, HD), lambda h: (0, 0, h)),
-            pl.BlockSpec((1, HD), lambda h: (0, h)),
-        ],
-        out_specs=(
-            pl.BlockSpec((all_rows, HD), lambda h: (0, h)),
-            pl.BlockSpec((all_rows, HD), lambda h: (0, 0)),
-        ),
-        compiler_params=pltpu.CompilerParams(
-            dimension_semantics=("arbitrary",), vmem_limit_bytes=VMEM_LIMIT
-        ),
-        name="attend",
-    )(qkv, gain)
-
-    out = pl.pallas_call(
-        functools.partial(scatter_kernel, n, float(n * head_cols)),
-        out_shape=jax.ShapeDtypeStruct((rows, width), BF16),
-        in_specs=[vm, vm, hbm, vm, vm],
-        out_specs=vm,
-        scratch_shapes=[
-            pltpu.VMEM((2, n * rows, cols), BF16),
-            pltpu.VMEM(w_out.shape, BF16),
-            pltpu.VMEM((n, rows, width), BF16),
-            pltpu.VMEM((n, rows, width), BF16),
-            pltpu.VMEM((rows, width), BF16),
-            pltpu.VMEM((2 * n, 8, 128), F32),
-            pltpu.VMEM((2 * n, 8, 128), F32),
-            dma(()),
-            dma(()),
-            dma(()),
-            dma(()),
+            regular,
+            regular,
+            dma((heads,)),
+            dma((heads,)),
+            dma((heads,)),
             dma((2 * n,)),
             dma((2 * n,)),
             dma((n,)),
@@ -627,10 +651,10 @@
             dma(()),
         ],
         compiler_params=pltpu.CompilerParams(
-            collective_id=1, has_side_effects=True, vmem_limit_bytes=VMEM_LIMIT
+            collective_id=0, has_side_effects=True, vmem_limit_bytes=VMEM_LIMIT
         ),
-        name="scatter",
-    )(att, power, wo, scale, x)
+        name="layer",
+    )(x, norm_gain.reshape(1, width), w, sub_gain.reshape(1, head_cols), w_out)
     return out[None]
 
 

time: 197 us -> 176 us (0.89)
  Pallas kernels: 189 us -> 171 us
    pallas_call x3 -> x1, Pallas kernels: 189 us -> 171 us  [body(): pl.pallas_call(functools.partial(layer_kernel, n, count, float(n * head_c...]
where the time goes in v2:
time: 176 us; the launch traced here: 174 us
  Pallas kernels  171 us (97%)
  local copies, waits for them, and re-layouts  2.29 us (1%)
    pallas_call x1, Pallas kernels, body(): pl.pallas_call(functools.partial(layer_kernel, n, count, float(n * head_c...  171 us

profile of v2, /device:TPU:15, one launch (start us, length us, event | category | flops | bytes accessed | tf_op | source)
XLA Modules:
  0.0 173.6 jit_solution(5996689953716591796)
XLA Ops:
  0.0 171.3 %layer.1 = bf16[128,4096]{1,0:T(8,128)(2,1)} custom-call(bf16[128,4096]{1,0:T(8,128)(2,1)} %bitcast.7, f32[1,4096]{1,0:T(1,128)} %bitcast.8, bf16[3,4096,1024]{2,1,0:T(8,128)(2,1)} %bitcast.5, f32[1,1024]{1,0:T(1,128)} %bitcast.9, bf16[1024,4096]{1,0:T(8,128)(2,1)} %wo_ref.1), custom_call_target="tpu_custom_call" | custom-call | tf_op jit(solution)/shard_map/layer/pallas_call | solution.py:615
  171.3 2.3 %copy.7 = bf16[1,128,4096]{2,1,0:T(8,128)(2,1)} copy(bf16[1,128,4096]{2,1,0:T(8,128)(2,1)} %bitcast.6) | data formatting | bytes 2097152

commit v3 on v2

--- a/solution.py
+++ b/solution.py
@@ -143,13 +143,18 @@
             device_id_type=MESH,
         )
 
-    @pl.when(z < n - 1)
-    def _():
-        to_right(z).start()
-
-    @pl.when(z > 0)
-    def _():
-        to_left(z).start()
+    def start_own():
+        @pl.when(z < n - 1)
+        def _():
+            to_right(z).start()
+
+        @pl.when(z > 0)
+        def _():
+            to_left(z).start()
+
+    @pl.when(c == 0)
+    def _():
+        start_own()
 
     to_partner(z).start()
 
@@ -209,7 +214,9 @@
 
             to_partner(owner).start()
 
-    forward(0)
+    @pl.when(c == 0)
+    def _():
+        forward(0)
 
     def get_tile(j, acc):
         tile_wait(n, c, z, part, sums, tile_send, tile_recv, j).wait_recv()
@@ -235,20 +242,33 @@
 
     block_rows = n * rows
 
-    def compute(owner):
-        from_partner(owner).wait_recv()
+    def compute(k, owner):
+        @pl.when(c != k)
+        def _():
+            from_partner(owner).wait_recv()
 
         def one(m, carry):
             s = scale_ref[pl.ds(m, 1), 0:1].astype(BF16).astype(F32)
-            y = jnp.dot(held[owner], w_held[m], preferred_element_type=F32) * s
-            y = y.astype(BF16)
-            qkv_ref[m, pl.ds(mult(owner * rows, 16), rows), :] = y[:rows]
-            qkv_ref[m, pl.ds(mult(block_rows + owner * rows, 16), rows), :] = y[rows:]
+            y = jnp.dot(
+                held[owner, k * rows : (k + 1) * rows, :], w_held[m], preferred_element_type=F32
+            )
+            at = pl.ds(mult(k * block_rows + owner * rows, 16), rows)
+            qkv_ref[m, at, :] = (y * s).astype(BF16)
             return carry
 
         lax.fori_loop(0, 3, one, 0)
 
-    compute(z)
+    def compute_at(k, s):
+        def side(u, carry):
+            owner = lax.select(u == 0, z - s, z + s)
+
+            @pl.when((owner >= 0) & (owner < n) & (u <= s))
+            def _():
+                compute(k, lax.rem(owner + n, n))
+
+            return carry
+
+        lax.fori_loop(0, 2, side, 0)
 
     def cut_out():
         half_o = jnp.broadcast_to((0.5 * scale_ref[3:4, 0:1]).astype(BF16), (16, width))
@@ -260,52 +280,32 @@
 
         lax.fori_loop(0, wo_held.shape[0] // 16, cut_o, 0)
 
-    def compute_both(s):
-        @pl.when(z - 1 - s >= 0)
-        def _():
-            compute(lax.rem(z - 1 - s + n, n))
-
-        @pl.when(z + 1 + s <= n - 1)
-        def _():
-            compute(lax.rem(z + 1 + s, n))
-
-    compute_both(0)
-    if n < 3:
-        cut_out()
-
-    def step(s, carry):
-        forward(s)
-        compute_both(s)
-
-        @pl.when(s == 1)
-        def _():
-            cut_out()
-
-        return carry
-
-    lax.fori_loop(1, n - 1, step, 0)
-
-    def finish(owner, carry):
-        @pl.when((owner <= z) & (z < n - 1))
-        def _():
-            to_right(owner).wait_send()
-
-        @pl.when((owner >= z) & (z > 0))
-        def _():
-            to_left(owner).wait_send()
-
-        to_partner(owner).wait_send()
-        return carry
-
-    lax.fori_loop(0, n, finish, 0)
-
-    @pl.when(z > 0)
-    def _():
-        pl.semaphore_signal(free_r, inc=1, device_id={"tp": lax.rem(z + n - 1, n)}, device_id_type=MESH)
-
-    @pl.when(z < n - 1)
-    def _():
-        pl.semaphore_signal(free_l, inc=1, device_id={"tp": lax.rem(z + 1, n)}, device_id_type=MESH)
+    def finish_sends():
+        def finish(owner, carry):
+            @pl.when((owner <= z) & (z < n - 1))
+            def _():
+                to_right(owner).wait_send()
+
+            @pl.when((owner >= z) & (z > 0))
+            def _():
+                to_left(owner).wait_send()
+
+            to_partner(owner).wait_send()
+            return carry
+
+        lax.fori_loop(0, n, finish, 0)
+
+        @pl.when(z > 0)
+        def _():
+            pl.semaphore_signal(
+                free_r, inc=1, device_id={"tp": lax.rem(z + n - 1, n)}, device_id_type=MESH
+            )
+
+        @pl.when(z < n - 1)
+        def _():
+            pl.semaphore_signal(
+                free_l, inc=1, device_id={"tp": lax.rem(z + 1, n)}, device_id_type=MESH
+            )
 
     mine_rows = pl.ds(mult(c * block_rows, 16), block_rows)
     their_rows = pl.ds(mult((1 - c) * block_rows, 16), block_rows)
@@ -331,8 +331,10 @@
     )
     turn = (((1,), (1,)), ((), ()))
     power_ref[...] = jnp.zeros_like(power_ref)
-
-    def head(h, carry):
+    heads = cols // HD
+    half = block_rows // block
+
+    def head(k, h):
         at = pl.ds(mult(h * HD, 128), HD)
         gain = sub_ref[:, pl.ds(mult(c * cols + h * HD, 128), HD)]
         def finish_rows(here, acc, total):
@@ -387,60 +389,54 @@
             finish_rows(here, acc, total)
             return carry
 
-        q_count = 2 * block_rows // block
-        if q_count <= 4:
-            for i in range(q_count):
+        if 2 * half <= 4:
+            for i in range(k * half, (k + 1) * half):
                 whole_rows(i)
         else:
-            lax.fori_loop(0, q_count, running_rows, 0)
-        swap(h).start()
-        keep(h).start()
-        return carry
-
-    heads = cols // HD
-    lax.fori_loop(0, heads, head, 0)
-
-    def sum_tile(b, carry):
-        ones = jnp.ones((8, 128), F32)
-        blk = power_ref[pl.ds(mult(b * rows, 8), rows), :]
-        tiles[b] = lax.dot_general(
-            ones, blk, (((1,), (1,)), ((), ())),
-            precision=lax.Precision.HIGHEST, preferred_element_type=F32,
-        )
-        return carry
-
-    lax.fori_loop(0, 2 * n, sum_tile, 0)
-    def send_power(j, carry):
-        other = lax.rem(c * n + z + j, 2 * n)
-        tile_copy(n, c, z, tiles.at[other], psums, ptile_send, ptile_recv, j).start()
-        return carry
-
-    lax.fori_loop(1, 2 * n, send_power, 0)
-
-    def arrived(h, carry):
-        keep(h).wait()
-        swap(h).wait_recv()
-        return carry
-
-    lax.fori_loop(0, heads, arrived, 0)
-
-    @pl.when(z > 0)
-    def _():
-        pl.semaphore_wait(free_l, 1)
-
-    @pl.when(z < n - 1)
-    def _():
-        pl.semaphore_wait(free_r, 1)
-
-    sum_at = pl.ds(0, rows)
-    got_at = pl.ds(rows, rows)
-
+            lax.fori_loop(k * half, (k + 1) * half, running_rows, 0)
+
+        @pl.when(c != k)
+        def _():
+            swap(h).start()
+
+        @pl.when(c == k)
+        def _():
+            keep(h).start()
+
+    flat = c * n + z
+
+    def attend(k):
+        def one_head(h, carry):
+            head(k, h)
+            return carry
+
+        lax.fori_loop(0, heads, one_head, 0)
+
+        def power_tile(j, carry):
+            b = k * n + j
+            ones = jnp.ones((8, 128), F32)
+            blk = power_ref[pl.ds(mult(b * rows, 8), rows), :]
+            tiles[b] = lax.dot_general(
+                ones, blk, (((1,), (1,)), ((), ())),
+                precision=lax.Precision.HIGHEST, preferred_element_type=F32,
+            )
+
+            @pl.when(b != flat)
+            def _():
+                step = lax.rem(b - flat + 2 * n, 2 * n)
+                tile_copy(n, c, z, tiles.at[b], psums, ptile_send, ptile_recv, step).start()
+
+            return carry
+
+        lax.fori_loop(0, n, power_tile, 0)
+
+    region = pl.ds(mine, rows)
     left = {"tp": lax.rem(z + n - 1, n)}
     right = {"tp": lax.rem(z + 1, n)}
 
     def move_sum(t, dst, recv, to):
         return pltpu.make_async_remote_copy(
-            src_ref=held.at[t, sum_at],
+            src_ref=held.at[t, region],
             dst_ref=dst,
             send_sem=send_sem.at[t],
             recv_sem=recv,
@@ -449,103 +445,161 @@
         )
 
     def sum_left(t):
-        return move_sum(t, held.at[t, got_at], recv_sem.at[t], left)
-
-    def to_right_pass(t):
-        return move_sum(t, held.at[t, got_at], recv_sem.at[t], right)
-
-    def to_right_last(t):
+        return move_sum(t, held.at[t, region], recv_sem.at[t], left)
+
+    def sum_right(t):
+        return move_sum(t, held.at[t, region], recv_sem.at[t], right)
+
+    def sum_right_last(t):
         return move_sum(t, extra, extra_sem, right)
 
-    def start_right(t):
+    def start_sum(t):
+        @pl.when(t < z)
+        def _():
+            sum_left(t).start()
+
         @pl.when(t == z + 1)
         def _():
-            to_right_last(t).start()
+            sum_right_last(t).start()
 
         @pl.when(t > z + 1)
         def _():
-            to_right_pass(t).start()
+            sum_right(t).start()
 
     tn = min(512, width)
-    scale_o = scale_ref[3:4, 0:1].astype(BF16).astype(F32)
-
-    def target(i):
-        return lax.select(2 * z >= n, i, n - 1 - i)
-
-    def first(i, carry):
-        t = target(i)
+
+    def product(t, there):
         at = pl.ds(mult(t * rows, 16), rows)
-
-        def cols_of(k, inner):
+        y = jnp.dot(a_held[0, at, :], wo_held[:cols, there], preferred_element_type=F32)
+        y = y + jnp.dot(a_held[1, at, :], wo_held[cols:, there], preferred_element_type=F32)
+        return (y * scale_ref[3:4, 0:1].astype(BF16).astype(F32)).astype(BF16)
+
+    def partial(t, add):
+        def cols_of(k, carry):
             there = pl.ds(mult(k * tn, 128), tn)
-            y = jnp.dot(a_held[0, at, :], wo_held[:cols, there], preferred_element_type=F32)
-            y = y + jnp.dot(a_held[1, at, :], wo_held[cols:, there], preferred_element_type=F32)
-            held[t, sum_at, there] = (y * scale_o).astype(BF16)
-            return inner
+            y = product(t, there)
+            if add:
+                y = (y.astype(F32) + held[t, region, there].astype(F32)).astype(BF16)
+            held[t, region, there] = y
+            return carry
 
         lax.fori_loop(0, width // tn, cols_of, 0)
 
-        @pl.when((z == n - 1) & (t < z))
-        def _():
-            sum_left(t).start()
-
-        @pl.when((z == 0) & (t > z))
-        def _():
-            start_right(t)
-
-        return carry
-
-    lax.fori_loop(0, n, first, 0)
-
-    def add_got(t):
-        def some(i, inner):
-            at = pl.ds(mult(i * 16, 16), 16)
-            there = pl.ds(mult(rows + i * 16, 16), 16)
-            held[t, at, :] = (
-                held[t, at, :].astype(F32) + held[t, there, :].astype(F32)
-            ).astype(BF16)
-            return inner
-
-        lax.fori_loop(0, rows // 16, some, 0)
-
-    def pass_left(t):
-        @pl.when((t < z) & (z < n - 1))
-        def _():
-            sum_left(t).wait_recv()
-            add_got(t)
-            sum_left(t).start()
-
-    def pass_right(t):
-        @pl.when((t > z) & (z > 0))
-        def _():
-            to_right_pass(t).wait_recv()
-            add_got(t)
-            start_right(t)
-
-    def second(i, carry):
-        @pl.when(2 * z >= n)
-        def _():
-            pass_left(i)
-
-        pass_right(n - 1 - i)
-
-        @pl.when(2 * z < n)
-        def _():
-            pass_left(i)
-
-        return carry
-
-    lax.fori_loop(0, n, second, 0)
-
-    def get_tile(j, acc):
+    def sums_begin():
+        def arrived(h, carry):
+            keep(h).wait()
+            swap(h).wait_recv()
+            return carry
+
+        lax.fori_loop(0, heads, arrived, 0)
+
+        @pl.when(z > 0)
+        def _():
+            pl.semaphore_wait(free_l, 1)
+
+        @pl.when(z < n - 1)
+        def _():
+            pl.semaphore_wait(free_r, 1)
+
+        def first(i, carry):
+            t = lax.select(2 * z >= n, i, n - 1 - i)
+
+            @pl.when(((z == n - 1) & (t < z)) | ((z == 0) & (t > z)))
+            def _():
+                partial(t, False)
+                start_sum(t)
+
+            return carry
+
+        lax.fori_loop(0, n, first, 0)
+
+    def sums_step(i):
+        def way(u, carry):
+            t = lax.select((2 * z >= n) == (u == 0), i, n - 1 - i)
+            is_left = (2 * z >= n) == (u == 0)
+
+            @pl.when((is_left & (t < z) & (z < n - 1)) | ((~is_left) & (t > z) & (z > 0)))
+            def _():
+                sum_left(t).wait_recv()
+                partial(t, True)
+                start_sum(t)
+
+            return carry
+
+        lax.fori_loop(0, 2, way, 0)
+
+    compute_at(0, 0)
+    compute_at(0, 1)
+    if n < 3:
+        cut_out()
+
+    def step(s, carry):
+        @pl.when(c == 0)
+        def _():
+            forward(s - 1)
+
+        compute_at(0, s)
+
+        @pl.when(s == 2)
+        def _():
+            cut_out()
+
+        return carry
+
+    lax.fori_loop(2, n, step, 0)
+
+    @pl.when(c == 1)
+    def _():
+        start_own()
+
+    @pl.when(c == 0)
+    def _():
+        finish_sends()
+
+    attend(0)
+
+    @pl.when(c == 0)
+    def _():
+        sums_begin()
+
+    def step_one(s, carry):
+        @pl.when((c == 1) & (s >= 1))
+        def _():
+            forward(s - 1)
+
+        compute_at(1, s)
+
+        @pl.when(c == 0)
+        def _():
+            sums_step(s)
+
+        return carry
+
+    lax.fori_loop(0, n, step_one, 0)
+
+    @pl.when(c == 1)
+    def _():
+        finish_sends()
+
+    attend(1)
+
+    @pl.when(c == 1)
+    def _():
+        sums_begin()
+
+        def step_two(s, carry):
+            sums_step(s)
+            return carry
+
+        lax.fori_loop(0, n, step_two, 0)
+
+    def get_power(j, acc):
         tile_wait(n, c, z, tiles.at[0], psums, ptile_send, ptile_recv, j).wait_recv()
-        return acc + psums[lax.rem(c * n + z + j, 2 * n)]
-
-    power = lax.fori_loop(1, 2 * n, get_tile, tiles[c * n + z]) / width_all
+        return acc + psums[lax.rem(flat + j, 2 * n)]
+
+    power = lax.fori_loop(1, 2 * n, get_power, tiles[flat]) / width_all
     r = lax.rsqrt(power[0:1, :] + eps_norm)
     r_col = jnp.transpose(jnp.broadcast_to(r, (rows, rows)))
-    tiles_of = width // rows
-    sums_r = r_col
 
     @pl.when(z < n - 1)
     def _():
@@ -553,32 +607,30 @@
 
     @pl.when(z > 0)
     def _():
-        to_right_last(z).wait_recv()
+        sum_right_last(z).wait_recv()
 
     @pl.when(z == n - 1)
     def _():
-        held[z, got_at, :] = jnp.zeros((rows, width), BF16)
+        held[z, region, :] = jnp.zeros((rows, width), BF16)
 
     @pl.when(z == 0)
     def _():
         extra[...] = jnp.zeros((rows, width), BF16)
 
+    r_wide = jnp.concatenate([r_col] * (tn // rows), axis=1)
+
     def last(k, carry):
-        at = pl.ds(mult(k * rows, 128), rows)
-        y = held[z, sum_at, at].astype(F32) + held[z, got_at, at].astype(F32) + extra[:, at].astype(F32)
-        out_ref[:, at] = (x_ref[:, at].astype(F32) + y * sums_r).astype(BF16)
-        return carry
-
-    lax.fori_loop(0, tiles_of, last, 0)
+        at = pl.ds(mult(k * tn, 128), tn)
+        y = product(z, at).astype(F32) + held[z, region, at].astype(F32) + extra[:, at].astype(F32)
+        out_ref[:, at] = (x_ref[:, at].astype(F32) + y * r_wide).astype(BF16)
+        return carry
+
+    lax.fori_loop(0, width // tn, last, 0)
 
     def finish_sum(t, carry):
-        @pl.when(t < z)
+        @pl.when(t != z)
         def _():
             sum_left(t).wait_send()
-
-        @pl.when(t > z)
-        def _():
-            to_right_pass(t).wait_send()
 
         return carry
 

time: 176 us -> 169 us (0.960); the launches traced: 174 us -> 169 us
  Pallas kernels: 171 us -> 166 us
    pallas_call x1, Pallas kernels: 171 us -> 166 us  [body(): pl.pallas_call(functools.partial(layer_kernel, n, count, float(n * head_c...]
where the time goes in v3:
time: 169 us
  Pallas kernels  166 us (98%)
  local copies, waits for them, and re-layouts  2.29 us (1%)
    pallas_call x1, Pallas kernels, body(): pl.pallas_call(functools.partial(layer_kernel, n, count, float(n * head_c...  166 us

profile of v3, /device:TPU:15, one launch (start us, length us, event | category | flops | bytes accessed | tf_op | source)
XLA Modules:
  0.0 168.6 jit_solution(1379985928692333384)
XLA Ops:
  0.0 166.3 %layer.1 = bf16[128,4096]{1,0:T(8,128)(2,1)} custom-call(bf16[128,4096]{1,0:T(8,128)(2,1)} %bitcast.7, f32[1,4096]{1,0:T(1,128)} %bitcast.8, bf16[3,4096,1024]{2,1,0:T(8,128)(2,1)} %bitcast.5, f32[1,1024]{1,0:T(1,128)} %bitcast.9, bf16[1024,4096]{1,0:T(8,128)(2,1)} %wo_ref.1), custom_call_target="tpu_custom_call" | custom-call | tf_op jit(solution)/shard_map/layer/pallas_call | solution.py:667
  166.3 2.3 %copy.7 = bf16[1,128,4096]{2,1,0:T(8,128)(2,1)} copy(bf16[1,128,4096]{2,1,0:T(8,128)(2,1)} %bitcast.6) | data formatting | bytes 2097152

commit v4 on v3

--- a/solution.py
+++ b/solution.py
@@ -530,6 +530,11 @@
 
     compute_at(0, 0)
     compute_at(0, 1)
+
+    @pl.when(c == 1)
+    def _():
+        start_own()
+
     if n < 3:
         cut_out()
 
@@ -547,10 +552,6 @@
         return carry
 
     lax.fori_loop(2, n, step, 0)
-
-    @pl.when(c == 1)
-    def _():
-        start_own()
 
     @pl.when(c == 0)
     def _():

time: 169 us -> 161 us (0.953)
  Pallas kernels: 166 us -> 159 us
    pallas_call x1, Pallas kernels: 166 us -> 159 us  [body(): pl.pallas_call(functools.partial(layer_kernel, n, count, float(n * head_c...]
where the time goes in v4:
time: 161 us
  Pallas kernels  159 us (99%)
  local copies, waits for them, and re-layouts  2.29 us (1%)
    pallas_call x1, Pallas kernels, body(): pl.pallas_call(functools.partial(layer_kernel, n, count, float(n * head_c...  159 us

profile of v4, /device:TPU:15, one launch (start us, length us, event | category | flops | bytes accessed | tf_op | source)
XLA Modules:
  0.0 161.2 jit_solution(4712523641214756964)
XLA Ops:
  0.0 158.9 %layer.1 = bf16[128,4096]{1,0:T(8,128)(2,1)} custom-call(bf16[128,4096]{1,0:T(8,128)(2,1)} %bitcast.7, f32[1,4096]{1,0:T(1,128)} %bitcast.8, bf16[3,4096,1024]{2,1,0:T(8,128)(2,1)} %bitcast.5, f32[1,1024]{1,0:T(1,128)} %bitcast.9, bf16[1024,4096]{1,0:T(8,128)(2,1)} %wo_ref.1), custom_call_target="tpu_custom_call" | custom-call | tf_op jit(solution)/shard_map/layer/pallas_call | solution.py:668
  158.9 2.3 %copy.7 = bf16[1,128,4096]{2,1,0:T(8,128)(2,1)} copy(bf16[1,128,4096]{2,1,0:T(8,128)(2,1)} %bitcast.6) | data formatting | bytes 2097152
